TPU v7x, 256 devices: a whole 4x4x8 slice. The times are simulated.
256 devices in a mesh: leaf: 32 (over x, z), sub: 8 (over y, core).
Axes of the slice: x: 4, y: 4, z: 8, core: 2. Of those that a mesh axis runs over, the one named last changes fastest.
Arguments:
- leaf_right: bfloat16 [1024, 512, 256], P(('leaf', 'sub')), may hold values from -6 to 6
- leaf_inverse: bfloat16 [1024, 512, 512], P(('leaf', 'sub')), may hold values from -2.5 to 2.5, as said below
- panels: bfloat16 [1024, 256, 512], P(('leaf', 'sub')), may hold values from -0.125 to 0.125
- leaf_subtree: int32 [1024], P(('leaf', 'sub')), may hold values from 0 to 31, as said below
- panel_block: int32 [1024, 4], P(('leaf', 'sub')), may hold values from 0 to 63
- separator_right: bfloat16 [131072, 256], P(('leaf', 'sub')), may hold values from -6 to 6
- separator_inverse: bfloat16 [131072, 512], P(('leaf', 'sub')), may hold values from -2.5 to 2.5, as said below
- separator_factor: bfloat16 [131072, 4096], P(('leaf', 'sub')), may hold values from -1 to 1, as said below
Outputs:
- leaf_solution: bfloat16 [1024, 512, 256], P(('leaf', 'sub'))
- separator_solution: bfloat16 [131072, 256], P(('leaf', 'sub'))
Inputs may be any that keep to these rules, and one draw needn't show every extreme that they name: `leaf_subtree`: every leaf supernode held by section s of the leaf axis belongs to a subtree between s - (2) and s. Each device of section s holds, for every d from 0 to min(2, s), at least one leaf supernode of subtree s - d. `leaf_inverse`: each 512 x 512 block is lower triangular, with its diagonal between 0.6 and 1.4. `separator_inverse`: each 512 x 512 block is lower triangular, with its diagonal between 0.6 and 1.4. `separator_factor`: within each subtree's 4096 rows, the block of row block q and column block p (blocks of 512) is zero unless q > p.
All inputs are finite; a program needn't handle non-finite values.
Results may differ from a plain program's by a relative error of at most 0.024.
Values may be sent and summed in bfloat16 or wider, within the bound.
No kernel may reach another device: no remote copies, remote signals or barrier semaphores. Data moves between devices by JAX's collectives and lax.ppermute only.
A program may use at most 128 MiB of HBM per device.

v0:
```python
import jax
import jax.numpy as jnp
from jax import lax
from jax.sharding import PartitionSpec as P

WSN = 512
SA = 4096
R = 256
BLK = 64
KB = 4
SPAN = 3
exact_precision = lax.Precision.HIGHEST


def passed_along(block, axis, distance):
    devices = range(lax.axis_size(axis))
    route = [(i - distance, i) for i in devices if i - distance in devices]
    return lax.ppermute(block, axis, route)


def broadcast(shard, axis, root):
    mine = lax.axis_index(axis) == root
    return lax.psum(jnp.where(mine, shard, jnp.zeros_like(shard)), axis)


def route_forward(stacked):
    summed = stacked[0]
    for distance in range(1, SPAN):
        summed = summed + passed_along(stacked[distance], "leaf", -distance)
    return summed


def route_back(item):
    collected = [item] + [passed_along(item, "leaf", distance) for distance in range(1, SPAN)]
    return jnp.stack(collected)


def shards(
    leaf_right,
    leaf_inverse,
    panels,
    leaf_subtree,
    panel_block,
    separator_right,
    separator_inverse,
    separator_factor,
):
    section = lax.axis_index("leaf")
    member = lax.axis_index("sub")
    leaves_here = leaf_right.shape[0]
    row_blocks = SA // BLK
    share_rows = separator_right.shape[0]
    per_device = share_rows // WSN
    solved = jnp.einsum(
        "jab,jbr->jar", leaf_inverse, leaf_right, preferred_element_type=jnp.float32
    ).astype(jnp.bfloat16)
    updates = jnp.einsum(
        "jib,jbr->jir", panels, solved, preferred_element_type=jnp.float32
    ).reshape(leaves_here * KB, BLK * R)
    offsets = section - leaf_subtree
    slot_index = (offsets[:, None] * row_blocks + panel_block).reshape(-1)
    selector = (
        jnp.arange(SPAN * row_blocks, dtype=jnp.int32)[:, None] == slot_index[None, :]
    ).astype(jnp.float32)
    spilled = jnp.dot(
        selector, updates, precision=exact_precision, preferred_element_type=jnp.float32
    ).reshape(SPAN, SA, R)
    own_rows = lax.psum_scatter(route_forward(spilled), "sub", scatter_dimension=0, tiled=True)
    rhs_rows = (separator_right.astype(jnp.float32) - own_rows).astype(jnp.bfloat16)
    inverse_blocks = separator_inverse.reshape(per_device, WSN, WSN)
    running = rhs_rows.astype(jnp.float32).reshape(per_device, WSN, R)
    empty_block = jnp.zeros((WSN, R), jnp.bfloat16)
    forward_store = jnp.zeros((per_device, WSN, R), jnp.bfloat16)
    for column in range(SA // WSN):
        owner = column // per_device
        local_col = column % per_device
        is_owner = member == owner

        def solve_block():
            return jnp.dot(
                inverse_blocks[local_col].astype(jnp.float32),
                running[local_col],
                precision=exact_precision,
                preferred_element_type=jnp.float32,
            ).astype(jnp.bfloat16)

        own_block = lax.cond(is_owner, solve_block, lambda: empty_block)
        block_y = broadcast(own_block, "sub", owner)
        forward_store = forward_store.at[local_col].set(
            jnp.where(is_owner, block_y, forward_store[local_col])
        )
        column_panel = separator_factor[:, column * WSN : (column + 1) * WSN]
        running = running - jnp.dot(
            column_panel, block_y, preferred_element_type=jnp.float32
        ).reshape(per_device, WSN, R)
    backward_store = jnp.zeros((per_device, WSN, R), jnp.bfloat16)
    for column in reversed(range(SA // WSN)):
        owner = column // per_device
        local_col = column % per_device
        is_owner = member == owner
        column_panel = separator_factor[:, column * WSN : (column + 1) * WSN]
        partial_term = lax.dot_general(
            column_panel,
            backward_store.reshape(share_rows, R),
            (((0,), (0,)), ((), ())),
            preferred_element_type=jnp.float32,
        )
        summed_later = lax.psum(partial_term, "sub")

        def back_block():
            bracket = forward_store[local_col].astype(jnp.float32) - summed_later
            return lax.dot_general(
                inverse_blocks[local_col].astype(jnp.float32),
                bracket,
                (((0,), (0,)), ((), ())),
                precision=exact_precision,
                preferred_element_type=jnp.float32,
            ).astype(jnp.bfloat16)

        own_back = lax.cond(is_owner, back_block, lambda: empty_block)
        backward_store = backward_store.at[local_col].set(
            jnp.where(is_owner, own_back, backward_store[local_col])
        )
    separator_x = backward_store.reshape(share_rows, R)
    solution_table = route_back(lax.all_gather(separator_x, "sub", axis=0, tiled=True))
    pieces = jnp.take(solution_table.reshape(SPAN * row_blocks, BLK * R), slot_index, axis=0)
    pieces = pieces.reshape(leaves_here, KB * BLK, R)
    reduced = jnp.einsum("jib,jir->jbr", panels, pieces, preferred_element_type=jnp.float32)
    inner_rhs = (solved.astype(jnp.float32) - reduced).astype(jnp.bfloat16)
    leaf_x = jnp.einsum(
        "jab,jar->jbr", leaf_inverse, inner_rhs, preferred_element_type=jnp.float32
    ).astype(jnp.bfloat16)
    return (leaf_x, separator_x)


def solution(mesh):
    placed = (
        P(("leaf", "sub"), None, None),
        P(("leaf", "sub"), None, None),
        P(("leaf", "sub"), None, None),
        P(("leaf", "sub")),
        P(("leaf", "sub"), None),
        P(("leaf", "sub"), None),
        P(("leaf", "sub"), None),
        P(("leaf", "sub"), None),
    )
    return jax.shard_map(
        shards,
        mesh=mesh,
        in_specs=placed,
        out_specs=(P(("leaf", "sub"), None, None), P(("leaf", "sub"), None)),
        check_vma=False,
    )
```

profile of v0, /device:TPU:34, one launch (start us, length us, event | category | flops | bytes accessed | tf_op | source)
XLA Modules:
  0.0 1701.3 jit_solution(7460126840667194432)
XLA Ops:
  8.9 2.0 convolution_convert_fusion.17
  13.4 2.6 copy.45
  16.0 2.4 reshape.570
  18.4 9.1 fusion.50
  27.5 9.4 fusion.57
  36.9 4.9 squeeze.31
  41.8 5.7 copy.46
  47.4 2.0 collective-permute-start
  49.4 5.0 squeeze.32
  54.4 5.6 copy.48
  60.1 8.2 collective-permute-start.1
  68.2 5.0 squeeze.29
  73.2 5.6 copy.47
  78.8 64.7 %collective-permute-done = f32[4096,256]{0,1:T(8,128)} collective-permute-done((f32[4096,256]{0,1:T(8,128)}, f32[4096,256]{0,1:T(8,128)}, u32[]{:S(2)}, u32[]{:S(2)}) %collective-permute-start) | collective-permute-done | bytes 4194336 | tf_op jit(solution)/shard_map/ppermute | solution.py:18
  143.6 91.9 %collective-permute-done.1 = f32[4096,256]{0,1:T(8,128)} collective-permute-done((f32[4096,256]{0,1:T(8,128)}, f32[4096,256]{0,1:T(8,128)}, u32[]{:S(2)}, u32[]{:S(2)}) %collective-permute-start.1) | collective-permute-done | bytes 4194336 | tf_op jit(solution)/shard_map/ppermute | solution.py:18
  235.5 7.8 add_add_fusion
  244.4 130.0 %reduce-scatter.2.cloned.1.call-done = f32[512,256]{0,1:T(8,128)} async-done(((f32[4096,256]{0,1:T(8,128)}), f32[512,256]{0,1:T(8,128)}) %reduce-scatter.2.cloned.1.call-update) | async-done | bytes 524304 | tf_op jit(solution)/shard_map/reduce_scatter | solution.py:68
  374.4 1.9 fusion.45
  376.4 1.7 conditional.16
  376.4 1.7 convolution_convert_fusion
  378.9 63.9 %all-reduce.17.cloned.1.call-done = bf16[512,256]{1,0:T(8,128)(2,1)} async-done(((bf16[512,256]{1,0:T(8,128)(2,1)}), bf16[512,256]{1,0:T(8,128)(2,1)}) %all-reduce.17.cloned.1.call-update) | async-done | bytes 262160 | tf_op jit(solution)/shard_map/psum | solution.py:23
  442.8 1.6 fusion.20
  445.3 64.7 %all-reduce.19.cloned.1.call-done = bf16[512,256]{1,0:T(8,128)(2,1)} async-done(((bf16[512,256]{1,0:T(8,128)(2,1)}), bf16[512,256]{1,0:T(8,128)(2,1)}) %all-reduce.19.cloned.1.call-update) | async-done | bytes 262160 | tf_op jit(solution)/shard_map/psum | solution.py:23
  510.0 2.3 fusion.21
  513.1 64.3 %all-reduce.21.cloned.1.call-done = bf16[512,256]{1,0:T(8,128)(2,1)} async-done(((bf16[512,256]{1,0:T(8,128)(2,1)}), bf16[512,256]{1,0:T(8,128)(2,1)}) %all-reduce.21.cloned.1.call-update) | async-done | bytes 262160 | tf_op jit(solution)/shard_map/psum | solution.py:23
  577.4 1.6 fusion.22
  580.1 64.4 %all-reduce.23.cloned.1.call-done = bf16[512,256]{1,0:T(8,128)(2,1)} async-done(((bf16[512,256]{1,0:T(8,128)(2,1)}), bf16[512,256]{1,0:T(8,128)(2,1)}) %all-reduce.23.cloned.1.call-update) | async-done | bytes 262160 | tf_op jit(solution)/shard_map/psum | solution.py:23
  644.5 2.3 fusion.23
  647.6 64.2 %all-reduce.25.cloned.1.call-done = bf16[512,256]{1,0:T(8,128)(2,1)} async-done(((bf16[512,256]{1,0:T(8,128)(2,1)}), bf16[512,256]{1,0:T(8,128)(2,1)}) %all-reduce.25.cloned.1.call-update) | async-done | bytes 262160 | tf_op jit(solution)/shard_map/psum | solution.py:23
  711.8 1.6 fusion.24
  714.3 64.7 %all-reduce.27.cloned.1.call-done = bf16[512,256]{1,0:T(8,128)(2,1)} async-done(((bf16[512,256]{1,0:T(8,128)(2,1)}), bf16[512,256]{1,0:T(8,128)(2,1)}) %all-reduce.27.cloned.1.call-update) | async-done | bytes 262160 | tf_op jit(solution)/shard_map/psum | solution.py:23
  779.0 2.3 fusion.25
  782.1 65.5 %all-reduce.29.cloned.1.call-done = bf16[512,256]{1,0:T(8,128)(2,1)} async-done(((bf16[512,256]{1,0:T(8,128)(2,1)}), bf16[512,256]{1,0:T(8,128)(2,1)}) %all-reduce.29.cloned.1.call-update) | async-done | bytes 262160 | tf_op jit(solution)/shard_map/psum | solution.py:23
  847.6 2.3 convolution_bitcast_fusion.9
  851.4 2.2 convolution_bitcast_fusion.8
  853.7 70.1 %all-reduce.31.cloned.1.call-done = bf16[512,256]{1,0:T(8,128)(2,1)} async-done(((bf16[512,256]{1,0:T(8,128)(2,1)}), bf16[512,256]{1,0:T(8,128)(2,1)}) %all-reduce.31.cloned.1.call-update) | async-done | bytes 262160 | tf_op jit(solution)/shard_map/psum | solution.py:23
  923.9 67.1 %all-reduce.33.cloned.1.call-done = f32[512,256]{0,1:T(8,128)} async-done(((f32[512,256]{0,1:T(8,128)}), f32[512,256]{0,1:T(8,128)}) %all-reduce.33.cloned.1.call-update) | async-done | bytes 524304 | tf_op jit(solution)/shard_map/psum | solution.py:108
  991.7 2.2 convolution_bitcast_fusion.7
  994.0 69.0 %all-reduce.35.cloned.1.call-done = f32[512,256]{0,1:T(8,128)} async-done(((f32[512,256]{0,1:T(8,128)}), f32[512,256]{0,1:T(8,128)}) %all-reduce.35.cloned.1.call-update) | async-done | bytes 524304 | tf_op jit(solution)/shard_map/psum | solution.py:108
  1063.8 2.2 convolution_bitcast_fusion.6
  1066.0 69.4 %all-reduce.37.cloned.1.call-done = f32[512,256]{0,1:T(8,128)} async-done(((f32[512,256]{0,1:T(8,128)}), f32[512,256]{0,1:T(8,128)}) %all-reduce.37.cloned.1.call-update) | async-done | bytes 524304 | tf_op jit(solution)/shard_map/psum | solution.py:108
  1135.4 2.3 convolution_bitcast_fusion.5
  1137.8 68.9 %all-reduce.39.cloned.1.call-done = f32[512,256]{0,1:T(8,128)} async-done(((f32[512,256]{0,1:T(8,128)}), f32[512,256]{0,1:T(8,128)}) %all-reduce.39.cloned.1.call-update) | async-done | bytes 524304 | tf_op jit(solution)/shard_map/psum | solution.py:108
  1207.4 2.2 convolution_bitcast_fusion.4
  1209.7 69.8 %all-reduce.41.cloned.1.call-done = f32[512,256]{0,1:T(8,128)} async-done(((f32[512,256]{0,1:T(8,128)}), f32[512,256]{0,1:T(8,128)}) %all-reduce.41.cloned.1.call-update) | async-done | bytes 524304 | tf_op jit(solution)/shard_map/psum | solution.py:108
  1279.6 2.3 convolution_bitcast_fusion.3
  1281.9 66.4 %all-reduce.43.cloned.1.call-done = f32[512,256]{0,1:T(8,128)} async-done(((f32[512,256]{0,1:T(8,128)}), f32[512,256]{0,1:T(8,128)}) %all-reduce.43.cloned.1.call-update) | async-done | bytes 524304 | tf_op jit(solution)/shard_map/psum | solution.py:108
  1349.1 2.2 convolution_bitcast_fusion.2
  1351.3 70.0 %all-reduce.45.cloned.1.call-done = f32[512,256]{0,1:T(8,128)} async-done(((f32[512,256]{0,1:T(8,128)}), f32[512,256]{0,1:T(8,128)}) %all-reduce.45.cloned.1.call-update) | async-done | bytes 524304 | tf_op jit(solution)/shard_map/psum | solution.py:108
  1421.3 2.2 convolution_bitcast_fusion.1
  1423.6 67.7 %all-reduce.47.cloned.1.call-done = f32[512,256]{0,1:T(8,128)} async-done(((f32[512,256]{0,1:T(8,128)}), f32[512,256]{0,1:T(8,128)}) %all-reduce.47.cloned.1.call-update) | async-done | bytes 524304 | tf_op jit(solution)/shard_map/psum | solution.py:108
  1491.3 5.5 conditional.31
  1491.3 2.1 copy.73
  1493.4 2.4 fusion.16
  1497.6 26.7 %all-gather.2.cloned.1.call-done = bf16[4096,256]{1,0:T(8,128)(2,1)} async-done(((bf16[512,256]{1,0:T(8,128)(2,1)}), bf16[4096,256]{1,0:T(8,128)(2,1)}) %all-gather.2.cloned.1.call-update) | async-done | bytes 2097168 | tf_op jit(solution)/shard_map/all_gather | solution.py:125
  1524.4 3.5 collective-permute-start.2
  1527.8 5.7 collective-permute-start.3
  1533.7 42.1 %collective-permute-done.2 = bf16[4096,256]{1,0:T(8,128)(2,1)} collective-permute-done((bf16[4096,256]{1,0:T(8,128)(2,1)}, bf16[4096,256]{1,0:T(8,128)(2,1)}, u32[]{:S(2)}, u32[]{:S(2)}) %collective-permute-start.2) | collective-permute-done | bytes 2097184 | tf_op jit(solution)/shard_map/ppermute | solution.py:18
  1575.9 90.4 %collective-permute-done.3 = bf16[4096,256]{1,0:T(8,128)(2,1)} collective-permute-done((bf16[4096,256]{1,0:T(8,128)(2,1)}, bf16[4096,256]{1,0:T(8,128)(2,1)}, u32[]{:S(2)}, u32[]{:S(2)}) %collective-permute-start.3) | collective-permute-done | bytes 2097184 | tf_op jit(solution)/shard_map/ppermute | solution.py:18
  1666.2 6.4 pad_maximum_fusion
  1672.7 10.5 reshape.571
  1683.2 4.9 gather_fusion
  1688.4 3.8 fusion.19
  1692.2 2.3 copy.76
  (105 shorter events, 22.4 us)
Async XLA Ops:
  7.2 1.7 copy-start
  7.2 367.2 %reduce-scatter.2.cloned.1.call-start = ((), (), s32[]{:S(2)}) async-start(), calls=%async_computation.1 | async-start | bytes 4718592 | tf_op jit(solution)/shard_map/reduce_scatter | solution.py:68
  8.9 3.0 copy-start.4
  10.9 1.0 copy-start.5
  47.4 96.2 %collective-permute-start = (f32[4096,256]{0,1:T(8,128)}, f32[4096,256]{0,1:T(8,128)}, u32[]{:S(2)}, u32[]{:S(2)}) collective-permute-start(f32[4096,256]{0,1:T(8,128)} %copy.46), channel_id=1, source_target_pairs={{8,0},{16,8},{24,16},{32,24},{40,32},{48,40},{56,48},{64,56},{72,6... | collective-permute-start | bytes 12582920 | tf_op jit(solution)/shard_map/ppermute | solution.py:18
  60.1 175.4 %collective-permute-start.1 = (f32[4096,256]{0,1:T(8,128)}, f32[4096,256]{0,1:T(8,128)}, u32[]{:S(2)}, u32[]{:S(2)}) collective-permute-start(f32[4096,256]{0,1:T(8,128)} %copy.48), channel_id=1, source_target_pairs={{16,0},{24,8},{32,16},{40,24},{48,32},{56,40},{64,48},{72,56},{80,... | collective-permute-start | bytes 12582920 | tf_op jit(solution)/shard_map/ppermute | solution.py:18
  243.3 0.9 copy-start.7
  243.3 133.0 %copy-start.1 = (bf16[512,512]{1,0:T(8,128)(2,1)S(1)}, bf16[512,512]{1,0:T(8,128)(2,1)}, u32[]{:S(2)}) copy-start(bf16[512,512]{1,0:T(8,128)(2,1)} %param.78) | copy-start | bytes 1572868
  243.3 199.4 %all-reduce.17.cloned.1.call-start = ((), (), s32[]{:S(2)}) async-start(), calls=%async_computation.2 | async-start | bytes 524288 | tf_op jit(solution)/shard_map/psum | solution.py:23
  378.8 131.2 %all-reduce.19.cloned.1.call-start = ((), (), s32[]{:S(2)}) async-start(), calls=%async_computation.3 | async-start | bytes 524288 | tf_op jit(solution)/shard_map/psum | solution.py:23
  445.2 132.2 %all-reduce.21.cloned.1.call-start = ((), (), s32[]{:S(2)}) async-start(), calls=%async_computation.4 | async-start | bytes 524288 | tf_op jit(solution)/shard_map/psum | solution.py:23
  513.0 131.4 %all-reduce.23.cloned.1.call-start = ((), (), s32[]{:S(2)}) async-start(), calls=%async_computation.5 | async-start | bytes 524288 | tf_op jit(solution)/shard_map/psum | solution.py:23
  580.0 131.8 %all-reduce.25.cloned.1.call-start = ((), (), s32[]{:S(2)}) async-start(), calls=%async_computation.6 | async-start | bytes 524288 | tf_op jit(solution)/shard_map/psum | solution.py:23
  647.5 131.5 %all-reduce.27.cloned.1.call-start = ((), (), s32[]{:S(2)}) async-start(), calls=%async_computation.7 | async-start | bytes 524288 | tf_op jit(solution)/shard_map/psum | solution.py:23
  714.2 133.4 %all-reduce.29.cloned.1.call-start = ((), (), s32[]{:S(2)}) async-start(), calls=%async_computation.8 | async-start | bytes 524288 | tf_op jit(solution)/shard_map/psum | solution.py:23
  782.0 141.7 %all-reduce.31.cloned.1.call-start = ((), (), s32[]{:S(2)}) async-start(), calls=%async_computation.9 | async-start | bytes 524288 | tf_op jit(solution)/shard_map/psum | solution.py:23
  782.1 141.7 %copy-start.6 = (bf16[512,256]{1,0:T(8,128)(2,1)S(1)}, bf16[512,256]{1,0:T(8,128)(2,1)}, u32[]{:S(2)}) copy-start(bf16[512,256]{1,0:T(8,128)(2,1)} %all-reduce.17.cloned.1.call-done) | copy-start | bytes 786436
  851.4 139.6 %all-reduce.33.cloned.1.call-start = ((), (), s32[]{:S(2)}) async-start(), calls=%async_computation.10 | async-start | bytes 1048576 | tf_op jit(solution)/shard_map/psum | solution.py:108
  853.6 209.4 %all-reduce.35.cloned.1.call-start = ((), (), s32[]{:S(2)}) async-start(), calls=%async_computation.11 | async-start | bytes 1048576 | tf_op jit(solution)/shard_map/psum | solution.py:108
  994.0 141.4 %all-reduce.37.cloned.1.call-start = ((), (), s32[]{:S(2)}) async-start(), calls=%async_computation.12 | async-start | bytes 1048576 | tf_op jit(solution)/shard_map/psum | solution.py:108
  1066.0 140.7 %all-reduce.39.cloned.1.call-start = ((), (), s32[]{:S(2)}) async-start(), calls=%async_computation.13 | async-start | bytes 1048576 | tf_op jit(solution)/shard_map/psum | solution.py:108
  1135.4 72.0 %copy-start.2 = (bf16[512,256]{1,0:T(8,128)(2,1)}, bf16[512,256]{1,0:T(8,128)(2,1)S(1)}, u32[]{:S(2)}) copy-start(bf16[512,256]{1,0:T(8,128)(2,1)S(1)} %get-tuple-element.460) | copy-start | bytes 786436
  1137.7 141.8 %all-reduce.41.cloned.1.call-start = ((), (), s32[]{:S(2)}) async-start(), calls=%async_computation.14 | async-start | bytes 1048576 | tf_op jit(solution)/shard_map/psum | solution.py:108
  1209.7 138.6 %all-reduce.43.cloned.1.call-start = ((), (), s32[]{:S(2)}) async-start(), calls=%async_computation.15 | async-start | bytes 1048576 | tf_op jit(solution)/shard_map/psum | solution.py:108
  1279.6 69.5 %copy-start.3 = (bf16[512,256]{1,0:T(8,128)(2,1)}, bf16[512,256]{1,0:T(8,128)(2,1)S(1)}, u32[]{:S(2)}) copy-start(bf16[512,256]{1,0:T(8,128)(2,1)S(1)} %get-tuple-element.462) | copy-start | bytes 786436
  1281.9 139.4 %all-reduce.45.cloned.1.call-start = ((), (), s32[]{:S(2)}) async-start(), calls=%async_computation.16 | async-start | bytes 1048576 | tf_op jit(solution)/shard_map/psum | solution.py:108
  1351.3 140.1 %all-reduce.47.cloned.1.call-start = ((), (), s32[]{:S(2)}) async-start(), calls=%async_computation.17 | async-start | bytes 1048576 | tf_op jit(solution)/shard_map/psum | solution.py:108
  1423.5 100.8 %all-gather.2.cloned.1.call-start = ((), (), s32[]{:S(2)}) async-start(), calls=%async_computation.18 | async-start | bytes 2359296 | tf_op jit(solution)/shard_map/all_gather | solution.py:125
  1524.4 51.5 %collective-permute-start.2 = (bf16[4096,256]{1,0:T(8,128)(2,1)}, bf16[4096,256]{1,0:T(8,128)(2,1)}, u32[]{:S(2)}, u32[]{:S(2)}) collective-permute-start(bf16[4096,256]{1,0:T(8,128)(2,1)} %all-gather.2.cloned.1.call-done), channel_id=1, source_target_pairs={{0,8},{8,16},{16,24},{24,32},{32,40},{40,48},{48,56},{56,64},{64,7... | collective-permute-start | bytes 6291464 | tf_op jit(solution)/shard_map/ppermute | solution.py:18
  1527.8 138.4 %collective-permute-start.3 = (bf16[4096,256]{1,0:T(8,128)(2,1)}, bf16[4096,256]{1,0:T(8,128)(2,1)}, u32[]{:S(2)}, u32[]{:S(2)}) collective-permute-start(bf16[4096,256]{1,0:T(8,128)(2,1)} %all-gather.2.cloned.1.call-done), channel_id=1, source_target_pairs={{0,16},{8,24},{16,32},{24,40},{32,48},{40,56},{48,64},{56,72},{64,... | collective-permute-start | bytes 6291464 | tf_op jit(solution)/shard_map/ppermute | solution.py:18
Sparse Core Ops, SparseCore 0:
  243.5 130.9 reduce-scatter.1
  378.9 63.8 all-reduce.16
  445.8 64.1 all-reduce.18
  513.1 64.2 all-reduce.20
  580.3 64.1 all-reduce.22
  647.6 64.1 all-reduce.24
  714.8 64.1 all-reduce.26
  782.2 65.4 all-reduce.28
  851.5 72.2 all-reduce.30
  926.0 65.0 all-reduce.32
  994.1 68.8 all-reduce.34
  1066.1 69.2 all-reduce.36
  1137.9 68.7 all-reduce.38
  1209.8 69.7 all-reduce.40
  1282.0 66.2 all-reduce.42
  1351.4 69.8 all-reduce.44
  1423.7 67.6 all-reduce.46
  1497.7 26.5 all-gather.1
where the time goes:
time: 1700 us
  waiting for transfers between devices  1520 us (89%)
  local copies, waits for them, and re-layouts  73.3 us (4%)
  matrix products  52.2 us (3%)
  other arithmetic  24.6 us (1%)
  starting transfers between devices  20 us (1%)
    psum x8, waiting for transfers between devices, shards(): summed_later = lax.psum(partial_term, 'sub')  548 us
    psum x8, waiting for transfers between devices, broadcast(): return lax.psum(jnp.where(mine, shard, jnp.zeros_like(shard)), axis)  522 us
    ppermute x4, waiting for transfers between devices, passed_along(): return lax.ppermute(block, axis, route)  289 us
    reduce_scatter x1, waiting for transfers between devices, shards(): lax.psum_scatter(route_forward(spilled), 'sub', scatter_dimension=0, tile...  130 us
  transfers between devices with their start and end apart: 22, of which 22 were waited for; matrix products, arithmetic and copies ran while one was open for 1% of the time, Pallas kernels for 0%

commit v1 on v0

--- a/solution.py
+++ b/solution.py
@@ -105,7 +105,7 @@
             (((0,), (0,)), ((), ())),
             preferred_element_type=jnp.float32,
         )
-        summed_later = lax.psum(partial_term, "sub")
+        summed_later = jnp.sum(lax.all_gather(partial_term, "sub"), axis=0)
 
         def back_block():
             bracket = forward_store[local_col].astype(jnp.float32) - summed_later

time: 1700 us -> 1520 us (0.89)
  waiting for transfers between devices: 1520 us -> 1320 us
    psum x8 -> x0, waiting for transfers between devices: 548 us -> none  [shards(): summed_later = lax.psum(partial_term, 'sub')]
    all_gather x0 -> x8, waiting for transfers between devices: none -> 356 us  [shards(): summed_later = jnp.sum(lax.all_gather(partial_term, 'sub'), axis=0)]
  transfers between devices with their start and end apart: 22 -> 22, of which waited for: 22 -> 22; matrix products, arithmetic and copies ran while one was open for 1% -> 2% of each run, Pallas kernels for 0% -> 0%
where the time goes in v1:
time: 1520 us
  waiting for transfers between devices  1320 us (87%)
  local copies, waits for them, and re-layouts  77 us (5%)
  matrix products  52.2 us (3%)
  other arithmetic  27.9 us (2%)
  starting transfers between devices  20.3 us (1%)
    psum x8, waiting for transfers between devices, broadcast(): return lax.psum(jnp.where(mine, shard, jnp.zeros_like(shard)), axis)  522 us
    all_gather x8, waiting for transfers between devices, shards(): summed_later = jnp.sum(lax.all_gather(partial_term, 'sub'), axis=0)  356 us
    ppermute x4, waiting for transfers between devices, passed_along(): return lax.ppermute(block, axis, route)  289 us
    reduce_scatter x1, waiting for transfers between devices, shards(): lax.psum_scatter(route_forward(spilled), 'sub', scatter_dimension=0, tile...  130 us
  transfers between devices with their start and end apart: 22, of which 22 were waited for; matrix products, arithmetic and copies ran while one was open for 2% of the time, Pallas kernels for 0%

profile of v1, /device:TPU:34, one launch (start us, length us, event | category | flops | bytes accessed | tf_op | source)
XLA Modules:
  0.0 1516.1 jit_solution(1771210512960494270)
XLA Ops:
  8.9 2.0 convolution_convert_fusion.17
  13.4 2.6 copy.45
  16.0 2.4 reshape.570
  18.4 9.1 fusion.50
  27.5 9.4 fusion.57
  36.9 4.9 squeeze.31
  41.8 5.7 copy.46
  47.4 2.0 collective-permute-start
  49.4 5.0 squeeze.32
  54.4 5.6 copy.48
  60.1 8.2 collective-permute-start.1
  68.2 5.0 squeeze.29
  73.2 5.6 copy.47
  78.8 64.7 %collective-permute-done = f32[4096,256]{0,1:T(8,128)} collective-permute-done((f32[4096,256]{0,1:T(8,128)}, f32[4096,256]{0,1:T(8,128)}, u32[]{:S(2)}, u32[]{:S(2)}) %collective-permute-start) | collective-permute-done | bytes 4194336 | tf_op jit(solution)/shard_map/ppermute | solution.py:18
  143.6 91.9 %collective-permute-done.1 = f32[4096,256]{0,1:T(8,128)} collective-permute-done((f32[4096,256]{0,1:T(8,128)}, f32[4096,256]{0,1:T(8,128)}, u32[]{:S(2)}, u32[]{:S(2)}) %collective-permute-start.1) | collective-permute-done | bytes 4194336 | tf_op jit(solution)/shard_map/ppermute | solution.py:18
  235.5 7.8 add_add_fusion
  244.4 130.0 %reduce-scatter.2.cloned.1.call-done = f32[512,256]{0,1:T(8,128)} async-done(((f32[4096,256]{0,1:T(8,128)}), f32[512,256]{0,1:T(8,128)}) %reduce-scatter.2.cloned.1.call-update) | async-done | bytes 524304 | tf_op jit(solution)/shard_map/reduce_scatter | solution.py:68
  374.4 1.9 fusion.45
  376.4 1.7 conditional.16
  376.4 1.7 convolution_convert_fusion
  378.9 63.9 %all-reduce.9.cloned.1.call-done = bf16[512,256]{1,0:T(8,128)(2,1)} async-done(((bf16[512,256]{1,0:T(8,128)(2,1)}), bf16[512,256]{1,0:T(8,128)(2,1)}) %all-reduce.9.cloned.1.call-update) | async-done | bytes 262160 | tf_op jit(solution)/shard_map/psum | solution.py:23
  442.8 1.6 fusion.20
  445.3 64.7 %all-reduce.11.cloned.1.call-done = bf16[512,256]{1,0:T(8,128)(2,1)} async-done(((bf16[512,256]{1,0:T(8,128)(2,1)}), bf16[512,256]{1,0:T(8,128)(2,1)}) %all-reduce.11.cloned.1.call-update) | async-done | bytes 262160 | tf_op jit(solution)/shard_map/psum | solution.py:23
  510.0 2.3 fusion.21
  513.1 64.3 %all-reduce.13.cloned.1.call-done = bf16[512,256]{1,0:T(8,128)(2,1)} async-done(((bf16[512,256]{1,0:T(8,128)(2,1)}), bf16[512,256]{1,0:T(8,128)(2,1)}) %all-reduce.13.cloned.1.call-update) | async-done | bytes 262160 | tf_op jit(solution)/shard_map/psum | solution.py:23
  580.1 64.4 %all-reduce.15.cloned.1.call-done = bf16[512,256]{1,0:T(8,128)(2,1)} async-done(((bf16[512,256]{1,0:T(8,128)(2,1)}), bf16[512,256]{1,0:T(8,128)(2,1)}) %all-reduce.15.cloned.1.call-update) | async-done | bytes 262160 | tf_op jit(solution)/shard_map/psum | solution.py:23
  644.5 2.3 fusion.23
  647.6 64.2 %all-reduce.17.cloned.1.call-done = bf16[512,256]{1,0:T(8,128)(2,1)} async-done(((bf16[512,256]{1,0:T(8,128)(2,1)}), bf16[512,256]{1,0:T(8,128)(2,1)}) %all-reduce.17.cloned.1.call-update) | async-done | bytes 262160 | tf_op jit(solution)/shard_map/psum | solution.py:23
  711.8 1.6 fusion.24
  714.3 64.7 %all-reduce.19.cloned.1.call-done = bf16[512,256]{1,0:T(8,128)(2,1)} async-done(((bf16[512,256]{1,0:T(8,128)(2,1)}), bf16[512,256]{1,0:T(8,128)(2,1)}) %all-reduce.19.cloned.1.call-update) | async-done | bytes 262160 | tf_op jit(solution)/shard_map/psum | solution.py:23
  779.0 2.3 fusion.25
  782.1 65.5 %all-reduce.21.cloned.1.call-done = bf16[512,256]{1,0:T(8,128)(2,1)} async-done(((bf16[512,256]{1,0:T(8,128)(2,1)}), bf16[512,256]{1,0:T(8,128)(2,1)}) %all-reduce.21.cloned.1.call-update) | async-done | bytes 262160 | tf_op jit(solution)/shard_map/psum | solution.py:23
  847.6 2.3 convolution_bitcast_fusion.9
  851.4 2.2 convolution_bitcast_fusion.8
  853.7 70.1 %all-reduce.23.cloned.1.call-done = bf16[512,256]{1,0:T(8,128)(2,1)} async-done(((bf16[512,256]{1,0:T(8,128)(2,1)}), bf16[512,256]{1,0:T(8,128)(2,1)}) %all-reduce.23.cloned.1.call-update) | async-done | bytes 262160 | tf_op jit(solution)/shard_map/psum | solution.py:23
  923.9 35.4 %all-gather.20.cloned.1.call-done = f32[4096,256]{0,1:T(8,128)} async-done(((f32[512,256]{0,1:T(8,128)}), f32[4096,256]{0,1:T(8,128)}) %all-gather.20.cloned.1.call-update) | async-done | bytes 4194320 | tf_op jit(solution)/shard_map/all_gather | solution.py:108
  960.1 2.2 convolution_bitcast_fusion.7
  962.3 44.5 %all-gather.22.cloned.1.call-done = f32[4096,256]{0,1:T(8,128)} async-done(((f32[512,256]{0,1:T(8,128)}), f32[4096,256]{0,1:T(8,128)}) %all-gather.22.cloned.1.call-update) | async-done | bytes 4194320 | tf_op jit(solution)/shard_map/all_gather | solution.py:108
  1007.6 2.2 convolution_bitcast_fusion.6
  1009.8 45.5 %all-gather.24.cloned.1.call-done = f32[4096,256]{0,1:T(8,128)} async-done(((f32[512,256]{0,1:T(8,128)}), f32[4096,256]{0,1:T(8,128)}) %all-gather.24.cloned.1.call-update) | async-done | bytes 4194320 | tf_op jit(solution)/shard_map/all_gather | solution.py:108
  1055.3 2.3 convolution_bitcast_fusion.5
  1057.7 47.1 %all-gather.26.cloned.1.call-done = f32[4096,256]{0,1:T(8,128)} async-done(((f32[512,256]{0,1:T(8,128)}), f32[4096,256]{0,1:T(8,128)}) %all-gather.26.cloned.1.call-update) | async-done | bytes 4194320 | tf_op jit(solution)/shard_map/all_gather | solution.py:108
  1105.6 2.2 convolution_bitcast_fusion.4
  1107.8 46.5 %all-gather.28.cloned.1.call-done = f32[4096,256]{0,1:T(8,128)} async-done(((f32[512,256]{0,1:T(8,128)}), f32[4096,256]{0,1:T(8,128)}) %all-gather.28.cloned.1.call-update) | async-done | bytes 4194320 | tf_op jit(solution)/shard_map/all_gather | solution.py:108
  1154.4 2.3 convolution_bitcast_fusion.3
  1156.7 45.9 %all-gather.30.cloned.1.call-done = f32[4096,256]{0,1:T(8,128)} async-done(((f32[512,256]{0,1:T(8,128)}), f32[4096,256]{0,1:T(8,128)}) %all-gather.30.cloned.1.call-update) | async-done | bytes 4194320 | tf_op jit(solution)/shard_map/all_gather | solution.py:108
  1203.3 2.2 convolution_bitcast_fusion.2
  1205.6 45.3 %all-gather.32.cloned.1.call-done = f32[4096,256]{0,1:T(8,128)} async-done(((f32[512,256]{0,1:T(8,128)}), f32[4096,256]{0,1:T(8,128)}) %all-gather.32.cloned.1.call-update) | async-done | bytes 4194320 | tf_op jit(solution)/shard_map/all_gather | solution.py:108
  1250.9 2.2 convolution_bitcast_fusion.1
  1253.2 46.0 %all-gather.34.cloned.1.call-done = f32[4096,256]{0,1:T(8,128)} async-done(((f32[512,256]{0,1:T(8,128)}), f32[4096,256]{0,1:T(8,128)}) %all-gather.34.cloned.1.call-update) | async-done | bytes 4194320 | tf_op jit(solution)/shard_map/all_gather | solution.py:108
  1299.2 12.5 conditional.31
  1299.2 5.7 copy.111
  1304.8 3.3 reduce_sum.79
  1308.2 2.4 fusion.16
  1312.4 26.7 %all-gather.18.cloned.1.call-done = bf16[4096,256]{1,0:T(8,128)(2,1)} async-done(((bf16[512,256]{1,0:T(8,128)(2,1)}), bf16[4096,256]{1,0:T(8,128)(2,1)}) %all-gather.18.cloned.1.call-update) | async-done | bytes 2097168 | tf_op jit(solution)/shard_map/all_gather | solution.py:125
  1339.1 3.5 collective-permute-start.2
  1342.6 5.9 collective-permute-start.3
  1348.8 41.9 %collective-permute-done.2 = bf16[4096,256]{1,0:T(8,128)(2,1)} collective-permute-done((bf16[4096,256]{1,0:T(8,128)(2,1)}, bf16[4096,256]{1,0:T(8,128)(2,1)}, u32[]{:S(2)}, u32[]{:S(2)}) %collective-permute-start.2) | collective-permute-done | bytes 2097184 | tf_op jit(solution)/shard_map/ppermute | solution.py:18
  1390.6 90.4 %collective-permute-done.3 = bf16[4096,256]{1,0:T(8,128)(2,1)} collective-permute-done((bf16[4096,256]{1,0:T(8,128)(2,1)}, bf16[4096,256]{1,0:T(8,128)(2,1)}, u32[]{:S(2)}, u32[]{:S(2)}) %collective-permute-start.3) | collective-permute-done | bytes 2097184 | tf_op jit(solution)/shard_map/ppermute | solution.py:18
  1481.0 6.4 pad_maximum_fusion
  1487.5 10.5 reshape.571
  1498.0 4.9 gather_fusion
  1503.1 3.8 fusion.19
  1507.0 2.3 copy.76
  (106 shorter events, 24.1 us)
Async XLA Ops:
  7.2 1.7 copy-start
  7.2 367.2 %reduce-scatter.2.cloned.1.call-start = ((), (), s32[]{:S(2)}) async-start(), calls=%async_computation.1 | async-start | bytes 4718592 | tf_op jit(solution)/shard_map/reduce_scatter | solution.py:68
  8.9 3.0 copy-start.4
  10.9 1.0 copy-start.5
  47.4 96.2 %collective-permute-start = (f32[4096,256]{0,1:T(8,128)}, f32[4096,256]{0,1:T(8,128)}, u32[]{:S(2)}, u32[]{:S(2)}) collective-permute-start(f32[4096,256]{0,1:T(8,128)} %copy.46), channel_id=1, source_target_pairs={{8,0},{16,8},{24,16},{32,24},{40,32},{48,40},{56,48},{64,56},{72,6... | collective-permute-start | bytes 12582920 | tf_op jit(solution)/shard_map/ppermute | solution.py:18
  60.1 175.4 %collective-permute-start.1 = (f32[4096,256]{0,1:T(8,128)}, f32[4096,256]{0,1:T(8,128)}, u32[]{:S(2)}, u32[]{:S(2)}) collective-permute-start(f32[4096,256]{0,1:T(8,128)} %copy.48), channel_id=1, source_target_pairs={{16,0},{24,8},{32,16},{40,24},{48,32},{56,40},{64,48},{72,56},{80,... | collective-permute-start | bytes 12582920 | tf_op jit(solution)/shard_map/ppermute | solution.py:18
  243.3 0.9 copy-start.7
  243.3 133.0 %copy-start.1 = (bf16[512,512]{1,0:T(8,128)(2,1)S(1)}, bf16[512,512]{1,0:T(8,128)(2,1)}, u32[]{:S(2)}) copy-start(bf16[512,512]{1,0:T(8,128)(2,1)} %param.78) | copy-start | bytes 1572868
  243.3 199.4 %all-reduce.9.cloned.1.call-start = ((), (), s32[]{:S(2)}) async-start(), calls=%async_computation.2 | async-start | bytes 524288 | tf_op jit(solution)/shard_map/psum | solution.py:23
  378.8 131.2 %all-reduce.11.cloned.1.call-start = ((), (), s32[]{:S(2)}) async-start(), calls=%async_computation.3 | async-start | bytes 524288 | tf_op jit(solution)/shard_map/psum | solution.py:23
  445.2 132.2 %all-reduce.13.cloned.1.call-start = ((), (), s32[]{:S(2)}) async-start(), calls=%async_computation.4 | async-start | bytes 524288 | tf_op jit(solution)/shard_map/psum | solution.py:23
  513.0 131.4 %all-reduce.15.cloned.1.call-start = ((), (), s32[]{:S(2)}) async-start(), calls=%async_computation.5 | async-start | bytes 524288 | tf_op jit(solution)/shard_map/psum | solution.py:23
  580.0 131.8 %all-reduce.17.cloned.1.call-start = ((), (), s32[]{:S(2)}) async-start(), calls=%async_computation.6 | async-start | bytes 524288 | tf_op jit(solution)/shard_map/psum | solution.py:23
  647.5 131.5 %all-reduce.19.cloned.1.call-start = ((), (), s32[]{:S(2)}) async-start(), calls=%async_computation.7 | async-start | bytes 524288 | tf_op jit(solution)/shard_map/psum | solution.py:23
  714.2 133.4 %all-reduce.21.cloned.1.call-start = ((), (), s32[]{:S(2)}) async-start(), calls=%async_computation.8 | async-start | bytes 524288 | tf_op jit(solution)/shard_map/psum | solution.py:23
  782.0 141.8 %all-reduce.23.cloned.1.call-start = ((), (), s32[]{:S(2)}) async-start(), calls=%async_computation.9 | async-start | bytes 524288 | tf_op jit(solution)/shard_map/psum | solution.py:23
  782.1 141.7 %copy-start.6 = (bf16[512,256]{1,0:T(8,128)(2,1)S(1)}, bf16[512,256]{1,0:T(8,128)(2,1)}, u32[]{:S(2)}) copy-start(bf16[512,256]{1,0:T(8,128)(2,1)} %all-reduce.9.cloned.1.call-done) | copy-start | bytes 786436
  851.4 107.9 %all-gather.20.cloned.1.call-start = ((), (), s32[]{:S(2)}) async-start(), calls=%async_computation.11 | async-start | bytes 4718592 | tf_op jit(solution)/shard_map/all_gather | solution.py:108
  853.6 153.2 %all-gather.22.cloned.1.call-start = ((), (), s32[]{:S(2)}) async-start(), calls=%async_computation.12 | async-start | bytes 4718592 | tf_op jit(solution)/shard_map/all_gather | solution.py:108
  962.3 93.0 %all-gather.24.cloned.1.call-start = ((), (), s32[]{:S(2)}) async-start(), calls=%async_computation.13 | async-start | bytes 4718592 | tf_op jit(solution)/shard_map/all_gather | solution.py:108
  1009.8 95.0 %all-gather.26.cloned.1.call-start = ((), (), s32[]{:S(2)}) async-start(), calls=%async_computation.14 | async-start | bytes 4718592 | tf_op jit(solution)/shard_map/all_gather | solution.py:108
  1055.3 49.5 %copy-start.2 = (bf16[512,256]{1,0:T(8,128)(2,1)}, bf16[512,256]{1,0:T(8,128)(2,1)S(1)}, u32[]{:S(2)}) copy-start(bf16[512,256]{1,0:T(8,128)(2,1)S(1)} %get-tuple-element.478) | copy-start | bytes 786436
  1057.7 96.7 %all-gather.28.cloned.1.call-start = ((), (), s32[]{:S(2)}) async-start(), calls=%async_computation.15 | async-start | bytes 4718592 | tf_op jit(solution)/shard_map/all_gather | solution.py:108
  1107.8 94.8 %all-gather.30.cloned.1.call-start = ((), (), s32[]{:S(2)}) async-start(), calls=%async_computation.16 | async-start | bytes 4718592 | tf_op jit(solution)/shard_map/all_gather | solution.py:108
  1154.4 48.2 %copy-start.3 = (bf16[512,256]{1,0:T(8,128)(2,1)}, bf16[512,256]{1,0:T(8,128)(2,1)S(1)}, u32[]{:S(2)}) copy-start(bf16[512,256]{1,0:T(8,128)(2,1)S(1)} %get-tuple-element.482) | copy-start | bytes 786436
  1156.7 94.2 %all-gather.32.cloned.1.call-start = ((), (), s32[]{:S(2)}) async-start(), calls=%async_computation.17 | async-start | bytes 4718592 | tf_op jit(solution)/shard_map/all_gather | solution.py:108
  1205.5 93.6 %all-gather.34.cloned.1.call-start = ((), (), s32[]{:S(2)}) async-start(), calls=%async_computation.18 | async-start | bytes 4718592 | tf_op jit(solution)/shard_map/all_gather | solution.py:108
  1253.1 86.0 %all-gather.18.cloned.1.call-start = ((), (), s32[]{:S(2)}) async-start(), calls=%async_computation.10 | async-start | bytes 2359296 | tf_op jit(solution)/shard_map/all_gather | solution.py:125
  1339.1 51.5 %collective-permute-start.2 = (bf16[4096,256]{1,0:T(8,128)(2,1)}, bf16[4096,256]{1,0:T(8,128)(2,1)}, u32[]{:S(2)}, u32[]{:S(2)}) collective-permute-start(bf16[4096,256]{1,0:T(8,128)(2,1)} %all-gather.18.cloned.1.call-done), channel_id=1, source_target_pairs={{0,8},{8,16},{16,24},{24,32},{32,40},{40,48},{48,56},{56,64},{64,7... | collective-permute-start | bytes 6291464 | tf_op jit(solution)/shard_map/ppermute | solution.py:18
  1342.6 138.4 %collective-permute-start.3 = (bf16[4096,256]{1,0:T(8,128)(2,1)}, bf16[4096,256]{1,0:T(8,128)(2,1)}, u32[]{:S(2)}, u32[]{:S(2)}) collective-permute-start(bf16[4096,256]{1,0:T(8,128)(2,1)} %all-gather.18.cloned.1.call-done), channel_id=1, source_target_pairs={{0,16},{8,24},{16,32},{24,40},{32,48},{40,56},{48,64},{56,72},{64,... | collective-permute-start | bytes 6291464 | tf_op jit(solution)/shard_map/ppermute | solution.py:18
Sparse Core Ops, SparseCore 0:
  243.5 130.9 reduce-scatter.1
  378.9 63.8 all-reduce.8
  445.8 64.1 all-reduce.10
  513.1 64.2 all-reduce.12
  580.3 64.1 all-reduce.14
  647.6 64.1 all-reduce.16
  714.8 64.1 all-reduce.18
  782.2 65.4 all-reduce.20
  851.5 72.2 all-reduce.22
  925.5 33.8 all-gather.19
  962.4 44.3 all-gather.21
  1009.9 45.3 all-gather.23
  1057.8 46.9 all-gather.25
  1107.9 46.3 all-gather.27
  1156.8 45.7 all-gather.29
  1205.7 45.1 all-gather.31
  1253.2 45.8 all-gather.33
  1312.5 26.5 all-gather.17
